TPU v7x, 128 devices: a whole 4x4x4 slice. The times are simulated.
128 devices in a mesh: req: 4 (over z), tile: 8 (over y, core), span: 4 (over x).
Axes of the slice: x: 4, y: 4, z: 4, core: 2. Of those that a mesh axis runs over, the one named last changes fastest.
Arguments:
- latents: bfloat16 [32, 64, 128, 512], P(('req', 'span'), 'tile'), may hold values from -12 to 12
- frame_counts: int32 [4], replicated, may hold values from 1 to 16, 32 in all
- norm_gain: float32 [512], replicated, may hold values from 0.1 to 1.9
- norm_shift: float32 [512], replicated, may hold values from -3 to 3
- conv_weight: bfloat16 [3, 3, 3, 512, 512], replicated, may hold values from -0.0546875 to 0.0546875
- conv_bias: float32 [512], replicated, may hold values from -2 to 2
Outputs:
- decoded: bfloat16 [32, 64, 128, 512], P(('req', 'span'), 'tile')
Inputs may be any that keep to these rules, and one draw needn't show every extreme that they name: `frame_counts`: the 4 counts sum to 32, and the largest is exactly 16.
All inputs are finite; a program needn't handle non-finite values.
Results may differ from a plain program's by a relative error of at most 0.0031.
Values may be sent and summed in bfloat16 or wider, within the bound.
No kernel may reach another device: no remote copies, remote signals or barrier semaphores. Data moves between devices by JAX's collectives and lax.ppermute only.
A program may use at most 192 MiB of HBM per device.

v0:
```python
import jax
import jax.numpy as jnp
from jax import lax
from jax.sharding import PartitionSpec as P

GROUPS = 32
EPSILON = 1e-06


def extended_2(array, sides, width):
    for axis, dim in sides:
        count, length = (lax.axis_size(axis), array.shape[dim])
        up = [(i, (i + 1) % count) for i in range(count - 1)]
        down = [(j, i) for i, j in up]
        last = lax.slice_in_dim(array, length - width, length, axis=dim)
        leading = lax.slice_in_dim(array, 0, width, axis=dim)
        before = lax.ppermute(last, axis, up)
        after = lax.ppermute(leading, axis, down)
        array = jnp.concatenate([before, array, after], axis=dim)
    return array


def shifted(array, axis, by):
    count = lax.axis_size(axis)
    pairs = [(i, i + by) for i in range(count) if 0 <= i + by < count]
    return lax.ppermute(array, axis, pairs)


def membership(positions, request_start, request_end):
    return (positions[:, None] >= request_start[None, :]) & (
        positions[:, None] < request_end[None, :]
    )


def normalize(
    source, positions, request_start, request_end, group_mean, group_scale, norm_gain, norm_shift
):
    inside = membership(positions, request_start, request_end).astype(jnp.float32)
    per_group = source.shape[-1] // group_mean.shape[1]
    frame_mean = jnp.repeat(
        jnp.dot(inside, group_mean, precision=lax.Precision.HIGHEST), per_group, axis=1
    )
    frame_scale = jnp.repeat(
        jnp.dot(inside, group_scale, precision=lax.Precision.HIGHEST), per_group, axis=1
    )
    centred = (source.astype(jnp.float32) - frame_mean[:, None, None, :]) * frame_scale[
        :, None, None, :
    ]
    return jax.nn.silu(centred * norm_gain + norm_shift).astype(jnp.bfloat16)


def finish_stats(local_sums, local_squares, cell_count):
    total_sums, total_squares = lax.psum((local_sums, local_squares), ("req", "tile", "span"))
    group_mean = total_sums / cell_count
    group_scale = lax.rsqrt(total_squares / cell_count - group_mean * group_mean + EPSILON)
    return (group_mean, group_scale)


def extend_rows(source):
    haloed = extended_2(source, (("tile", 1),), 1)
    tile_place = lax.axis_index("tile")
    upper_rim = jnp.where(tile_place == 0, haloed[:, 1:2], haloed[:, 0:1])
    bottom = jnp.where(tile_place == lax.axis_size("tile") - 1, haloed[:, -2:-1], haloed[:, -1:])
    return jnp.concatenate([upper_rim, haloed[:, 1:-1], bottom], axis=1)


def extend_frames(source):
    earlier = shifted(source, ("req", "span"), 1)
    return jnp.concatenate([earlier, source], axis=0)


def extend(source):
    grown = extend_rows(extend_frames(source))
    return grown


def convolve(padded, tap_index, conv_weight, frame_count, row_count, col_count, channels):
    accumulated = jnp.zeros((frame_count * row_count * col_count, channels), jnp.float32)
    for time_tap in range(3):
        chosen = jnp.take(padded, tap_index[time_tap], axis=0)
        for row_tap in range(3):
            stacked = jnp.concatenate(
                [
                    chosen[:, row_tap : row_tap + row_count, col_tap : col_tap + col_count]
                    for col_tap in range(3)
                ],
                axis=-1,
            )
            kernel = conv_weight[time_tap, row_tap].reshape(3 * channels, channels)
            accumulated = accumulated + jnp.dot(
                stacked.reshape(frame_count * row_count * col_count, 3 * channels),
                kernel,
                preferred_element_type=jnp.float32,
            )
    return accumulated.reshape(frame_count, row_count, col_count, channels)


def shards(latents, frame_counts, norm_gain, norm_shift, conv_weight, conv_bias):
    frame_count, row_count, col_count, channels = latents.shape
    per_group = channels // GROUPS
    request_end = jnp.cumsum(frame_counts)
    request_start = request_end - frame_counts
    first_frame = lax.axis_index(("req", "span")) * frame_count
    positions = first_frame + jnp.arange(frame_count, dtype=jnp.int32)
    inside = membership(positions, request_start, request_end)
    values = latents.astype(jnp.float32)
    group_sums = jnp.sum(values, axis=(1, 2)).reshape(frame_count, GROUPS, per_group).sum(-1)
    group_squares = (
        jnp.sum(values * values, axis=(1, 2)).reshape(frame_count, GROUPS, per_group).sum(-1)
    )
    weights_in = inside.astype(jnp.float32)
    local_sums = jnp.dot(weights_in.T, group_sums, precision=lax.Precision.HIGHEST)
    local_squares = jnp.dot(weights_in.T, group_squares, precision=lax.Precision.HIGHEST)
    cell_count = (
        frame_counts * (row_count * lax.axis_size("tile") * col_count * per_group)
    ).astype(jnp.float32)[:, None]
    group_mean, group_scale = finish_stats(local_sums, local_squares, cell_count)
    hidden = normalize(
        latents,
        positions,
        request_start,
        request_end,
        group_mean,
        group_scale,
        norm_gain,
        norm_shift,
    )
    extended = extend(hidden)
    padded = jnp.pad(extended, ((0, 0), (0, 0), (1, 1), (0, 0)), mode="edge")
    frame_start = jnp.sum(jnp.where(inside, request_start[None, :], 0), axis=1)
    tap_index = jnp.stack(
        [
            jnp.maximum(positions - 2 + time_tap, frame_start) - first_frame + 2
            for time_tap in range(3)
        ],
        axis=0,
    )
    conv = convolve(padded, tap_index, conv_weight, frame_count, row_count, col_count, channels)
    return (values + conv + conv_bias).astype(jnp.bfloat16)


def solution(mesh):
    placed = (P(("req", "span"), "tile", None, None), P(), P(), P(), P(), P())
    return jax.shard_map(
        shards,
        mesh=mesh,
        in_specs=placed,
        out_specs=P(("req", "span"), "tile", None, None),
        check_vma=False,
    )
```

profile of v0, /device:TPU:41, one launch (start us, length us, event | category | flops | bytes accessed | tf_op | source)
XLA Modules:
  0.0 287.2 jit_solution(3329410029690608245)
XLA Ops:
  4.6 65.0 %all-reduce = (f32[4,32]{1,0:T(4,128)S(1)}, f32[4,32]{1,0:T(4,128)S(1)}) all-reduce(f32[4,32]{1,0:T(4,128)S(1)} %fusion.40, f32[4,32]{1,0:T(4,128)S(1)} %fusion.39), channel_id=1, replica_groups=mesh['req'=4,'tile'=8,'span'=4] {'req','tile','span'}, use_global_device_ids=true, to_apply=%region_6.7 | all-reduce | flops 256 | bytes 2048 | tf_op jit(solution)/shard_map/psum | solution.py:53
  75.3 48.6 %collective-permute-done = bf16[2,8,128,512]{3,2,1,0:T(8,128)(2,1)} collective-permute-done((bf16[2,8,128,512]{3,2,1,0:T(8,128)(2,1)S(1)}, bf16[2,8,128,512]{3,2,1,0:T(8,128)(2,1)}, u32[]{:S(2)}, u32[]{:S(2)}) %collective-permute-start) | collective-permute-done | bytes 2097184 | tf_op jit(solution)/shard_map/ppermute | solution.py:26
  124.9 4.4 %collective-permute-start.1 = (bf16[4,1,128,512]{3,2,1,0:T(8,128)(2,1)S(1)}, bf16[4,1,128,512]{3,2,1,0:T(8,128)(2,1)S(1)}, u32[]{:S(2)}, u32[]{:S(2)}) collective-permute-start(bf16[4,1,128,512]{3,2,1,0:T(8,128)(2,1)S(1)} %pad_maximum_fusion.9), channel_id=1, source_target_pairs={{0,4},{4,8},{8,12},{12,16},{16,20},{20,24},{24,28},{1,5},{5,9},{9,... | collective-permute-start | bytes 1572872 | tf_op jit(solution)/shard_map/ppermute | solution.py:17
  129.4 6.0 %collective-permute-done.1 = bf16[4,1,128,512]{3,2,1,0:T(8,128)(2,1)S(1)} collective-permute-done((bf16[4,1,128,512]{3,2,1,0:T(8,128)(2,1)S(1)}, bf16[4,1,128,512]{3,2,1,0:T(8,128)(2,1)S(1)}, u32[]{:S(2)}, u32[]{:S(2)}) %collective-permute-start.1) | collective-permute-done | bytes 524320 | tf_op jit(solution)/shard_map/ppermute | solution.py:17
  140.1 9.6 %fusion.35 = (bf16[1,1,3,512,512]{4,3,2,1,0:T(8,128)(2,1)}, bf16[1,1,3,512,512]{4,3,2,1,0:T(8,128)(2,1)}, bf16[1,1,3,512,512]{4,3,2,1,0:T(8,128)(2,1)}, bf16[1,1...) fusion(bf16[3,3,3,512,512]{4,3,2,1,0:T(8,128)(2,1)} %param.12), kind=kLoop, calls=%fused_computation.77 | loop fusion | bytes 28311552 | tf_op jit(solution)/shard_map/slice | solution.py:89
  149.8 9.9 %fusion.11 = bf16[4,10,130,512]{3,2,1,0:T(8,128)(2,1)} fusion(bf16[4,1,128,512]{3,2,1,0:T(8,128)(2,1)S(1)} %broadcast_select_fusion.3, bf16[4,1,128,512]{3,2,1,0:T(8,128)(2,1)S(1)} %get-tuple-element.18, bf16[2,8,128,512]{3,2,1,0:T(8,128)(2,1)S(1)} %fusion.24, bf16[2,8,128,512]{3,2,1,0:T(8,128)(2,1)} %collective-permute-done), kind=kLoop, calls=%fused_computation.29 | loop fusion | flops 90521600 | bytes 10567680 | tf_op jit(solution)/shard_map/jit(_pad)/concatenate | solution.py:129
  163.0 4.9 %gather_fusion.1 = bf16[2,10,130,512]{3,2,1,0:T(8,128)(2,1)} fusion(bf16[4,10,130,512]{3,2,1,0:T(8,128)(2,1)} %fusion.11, s32[1024]{0:T(1024)S(1)} %pad_clamp_fusion.1), kind=kCustom, calls=%fused_computation.1.clone | custom fusion | bytes 5324808 | tf_op jit(solution)/shard_map/jit(_take)/gather | solution.py:80
  168.0 4.9 %gather_fusion = bf16[2,10,130,512]{3,2,1,0:T(8,128)(2,1)} fusion(bf16[4,10,130,512]{3,2,1,0:T(8,128)(2,1)} %fusion.11, s32[1024]{0:T(1024)S(1)} %pad_clamp_fusion.2), kind=kCustom, calls=%fused_computation.clone | custom fusion | bytes 5324808 | tf_op jit(solution)/shard_map/jit(_take)/gather | solution.py:80
  175.2 8.0 %fusion.36 = (bf16[2,8,128,512]{3,2,1,0:T(8,128)(2,1)}, bf16[2,8,128,512]{3,2,1,0:T(8,128)(2,1)}, bf16[2,8,128,512]{3,2,1,0:T(8,128)(2,1)}, bf16[2,8,128,512]{3,...) fusion(bf16[2,10,130,512]{3,2,1,0:T(8,128)(2,1)S(1)} %get-tuple, ...), kind=kLoop, calls=%fused_computation.78 | loop fusion | bytes 37748736 | tf_op jit(solution)/shard_map/slice | solution.py:84
  183.5 6.8 %fusion.37 = (bf16[2,8,128,512]{3,2,1,0:T(8,128)(2,1)S(1)}, bf16[2,8,128,512]{3,2,1,0:T(8,128)(2,1)}, bf16[2,8,128,512]{3,2,1,0:T(8,128)(2,1)}, bf16[2,8,128,512...) fusion(bf16[2,10,130,512]{3,2,1,0:T(8,128)(2,1)S(1)} %broadcast, ...), kind=kLoop, calls=%fused_computation.79 | loop fusion | bytes 37748736 | tf_op jit(solution)/shard_map/slice | solution.py:84
  190.3 7.1 %fusion.38 = (bf16[2,8,128,512]{3,2,1,0:T(8,128)(2,1)}, bf16[2,8,128,512]{3,2,1,0:T(8,128)(2,1)}, bf16[2,8,128,512]{3,2,1,0:T(8,128)(2,1)}, bf16[2,8,128,512]{3,...) fusion(bf16[2,10,130,512]{3,2,1,0:T(8,128)(2,1)S(1)} %get-tuple, ...), kind=kLoop, calls=%fused_computation.80 | loop fusion | bytes 37748736 | tf_op jit(solution)/shard_map/slice | solution.py:84
  201.1 4.9 %fusion.48 = f32[2048,512]{1,0:T(8,128)} fusion(bf16[2048,1536]{1,0:T(8,128)(2,1)S(1)} %bitcast.49, bf16[1536,512]{1,0:T(8,128)(2,1)S(1)} %bitcast.64), kind=kOutput, calls=%fused_computation.90 | convolution fusion | flops 3221225472 | bytes 12058624 | tf_op jit(solution)/shard_map/dot_general | solution.py:90
  206.0 4.4 %pad_maximum_fusion.6 = bf16[2,8,128,1536]{3,2,1,0:T(8,128)(2,1)S(1)} fusion(bf16[2,8,128,512]{3,2,1,0:T(8,128)(2,1)S(1)} %copy-done.17, bf16[2,8,128,512]{3,2,1,0:T(8,128)(2,1)S(1)} %copy-done.18, bf16[2,8,128,512]{3,2,1,0:T(8,128)(2,1)S(1)} %copy-done.19), kind=kLoop, calls=%fused_computation.23 | loop fusion | flops 18874368 | bytes 12582912 | tf_op jit(solution)/shard_map/concatenate | solution.py:82
  210.5 4.9 %fusion.47 = f32[2048,512]{1,0:T(8,128)} fusion(bf16[2048,1536]{1,0:T(8,128)(2,1)S(1)} %bitcast.50, bf16[1536,512]{1,0:T(8,128)(2,1)S(1)} %bitcast.63), kind=kOutput, calls=%fused_computation.89 | convolution fusion | flops 3221225472 | bytes 12058624 | tf_op jit(solution)/shard_map/dot_general | solution.py:90
  216.8 4.9 %fusion.41 = f32[2048,512]{1,0:T(8,128)} fusion(bf16[2048,1536]{1,0:T(8,128)(2,1)S(1)} %bitcast.56, bf16[1536,512]{1,0:T(8,128)(2,1)S(1)} %bitcast.62), kind=kOutput, calls=%fused_computation.83 | convolution fusion | flops 3221225472 | bytes 12058624 | tf_op jit(solution)/shard_map/dot_general | solution.py:90
  221.7 4.9 %fusion.42 = f32[2048,512]{1,0:T(8,128)} fusion(bf16[2048,1536]{1,0:T(8,128)(2,1)S(1)} %bitcast.55, bf16[1536,512]{1,0:T(8,128)(2,1)S(1)} %bitcast.61), kind=kOutput, calls=%fused_computation.84 | convolution fusion | flops 3221225472 | bytes 12058624 | tf_op jit(solution)/shard_map/dot_general | solution.py:90
  230.9 4.9 %fusion.43 = f32[2048,512]{1,0:T(8,128)} fusion(bf16[2048,1536]{1,0:T(8,128)(2,1)S(1)} %bitcast.51, bf16[1536,512]{1,0:T(8,128)(2,1)S(1)} %bitcast.60), kind=kOutput, calls=%fused_computation.85 | convolution fusion | flops 3221225472 | bytes 12058624 | tf_op jit(solution)/shard_map/dot_general | solution.py:90
  235.8 4.2 %pad_maximum_fusion.3 = bf16[2,8,128,1536]{3,2,1,0:T(8,128)(2,1)S(1)} fusion(bf16[2,8,128,512]{3,2,1,0:T(8,128)(2,1)S(1)} %copy-done.12, bf16[2,8,128,512]{3,2,1,0:T(8,128)(2,1)S(1)} %copy-done.13, bf16[2,8,128,512]{3,2,1,0:T(8,128)(2,1)S(1)} %copy-done.11), kind=kLoop, calls=%fused_computation.20 | loop fusion | flops 18874368 | bytes 12582912 | tf_op jit(solution)/shard_map/concatenate | solution.py:82
  240.1 4.9 %fusion.44 = f32[2048,512]{1,0:T(8,128)} fusion(bf16[2048,1536]{1,0:T(8,128)(2,1)S(1)} %bitcast.52, bf16[1536,512]{1,0:T(8,128)(2,1)S(1)} %bitcast.59), kind=kOutput, calls=%fused_computation.86 | convolution fusion | flops 3221225472 | bytes 12058624 | tf_op jit(solution)/shard_map/dot_general | solution.py:90
  249.3 4.9 %fusion.46 = f32[2048,512]{1,0:T(8,128)} fusion(bf16[2048,1536]{1,0:T(8,128)(2,1)S(1)} %bitcast.53, bf16[1536,512]{1,0:T(8,128)(2,1)S(1)} %bitcast.58), kind=kOutput, calls=%fused_computation.88 | convolution fusion | flops 3221225472 | bytes 12058624 | tf_op jit(solution)/shard_map/dot_general | solution.py:90
  254.3 4.5 %pad_maximum_fusion.4 = bf16[2,8,128,1536]{3,2,1,0:T(8,128)(2,1)S(1)} fusion(bf16[2,8,128,512]{3,2,1,0:T(8,128)(2,1)S(1)} %get-tuple-element.51, bf16[2,8,128,512]{3,2,1,0:T(8,128)(2,1)S(1)} %copy-done.6, bf16[2,8,128,512]{3,2,1,0:T(8,128)(2,1)S(1)} %copy-done.7), kind=kLoop, calls=%fused_computation.21 | loop fusion | flops 18874368 | bytes 12582912 | tf_op jit(solution)/shard_map/concatenate | solution.py:82
  258.8 5.0 %fusion.45 = f32[2048,512]{1,0:T(8,128)} fusion(bf16[2048,1536]{1,0:T(8,128)(2,1)S(1)} %bitcast.54, bf16[1536,512]{1,0:T(8,128)(2,1)S(1)} %bitcast.57), kind=kOutput, calls=%fused_computation.87 | convolution fusion | flops 3221225472 | bytes 12058624 | tf_op jit(solution)/shard_map/dot_general | solution.py:90
  268.0 14.8 %add_add_fusion = f32[2048,512]{1,0:T(8,128)} fusion(f32[2048,512]{1,0:T(8,128)} %fusion.48, f32[2048,512]{1,0:T(8,128)} %fusion.47, f32[2048,512]{1,0:T(8,128)} %fusion.46, f32[2048,512]{1,0:T(8,128)} %fusion.45, f32[2048,512]{1,0:T(8,128)} %fusion.44, f32[2048,512]{1,0:T(8,128)} %fusion.43, f32[2048,512]{1,0:T(8,128)} %fusion.41, ...), kind=kOutput, calls=%fused_computation.46 | convolution fusion | flops 3229614080 | bytes 45613056 | tf_op jit(solution)/shard_map/dot_general | solution.py:90
  282.8 4.4 %fusion.27 = bf16[2,8,128,512]{3,2,1,0:T(8,128)(2,1)} fusion(f32[2,8,128,512]{3,2,1,0:T(8,128)} %bitcast.47, bf16[2,8,128,512]{3,2,1,0:T(8,128)(2,1)S(1)} %copy-done, f32[512]{0:T(512)S(1)} %copy-done.28), kind=kLoop, calls=%fused_computation.45 | loop fusion | flops 4194304 | bytes 8390656 | tf_op jit(solution)/shard_map/convert_element_type | solution.py:139
  (94 shorter events, 39.8 us)
Async XLA Ops:
  73.4 50.6 %collective-permute-start = (bf16[2,8,128,512]{3,2,1,0:T(8,128)(2,1)S(1)}, bf16[2,8,128,512]{3,2,1,0:T(8,128)(2,1)}, u32[]{:S(2)}, u32[]{:S(2)}) collective-permute-start(bf16[2,8,128,512]{3,2,1,0:T(8,128)(2,1)S(1)} %fusion.24), channel_id=1, source_target_pairs={{0,1},{1,2},{2,3},{3,32},{32,33},{33,34},{34,35},{35,64},{64,65},{... | collective-permute-start | bytes 6291464 | tf_op jit(solution)/shard_map/ppermute | solution.py:26
  124.9 10.5 %collective-permute-start.1 = (bf16[4,1,128,512]{3,2,1,0:T(8,128)(2,1)S(1)}, bf16[4,1,128,512]{3,2,1,0:T(8,128)(2,1)S(1)}, u32[]{:S(2)}, u32[]{:S(2)}) collective-permute-start(bf16[4,1,128,512]{3,2,1,0:T(8,128)(2,1)S(1)} %pad_maximum_fusion.9), channel_id=1, source_target_pairs={{0,4},{4,8},{8,12},{12,16},{16,20},{20,24},{24,28},{1,5},{5,9},{9,... | collective-permute-start | bytes 1572872 | tf_op jit(solution)/shard_map/ppermute | solution.py:17
  136.5 13.2 %collective-permute-start.2 = (bf16[4,1,128,512]{3,2,1,0:T(8,128)(2,1)S(1)}, bf16[4,1,128,512]{3,2,1,0:T(8,128)(2,1)S(1)}, u32[]{:S(2)}, u32[]{:S(2)}) collective-permute-start(bf16[4,1,128,512]{3,2,1,0:T(8,128)(2,1)S(1)} %get-tuple-element.19), channel_id=1, source_target_pairs={{4,0},{8,4},{12,8},{16,12},{20,16},{24,20},{28,24},{5,1},{9,5},{13... | collective-permute-start | bytes 1572872 | tf_op jit(solution)/shard_map/ppermute | solution.py:18
  175.2 8.0 %copy-start.1 = (bf16[2,10,130,512]{3,2,1,0:T(8,128)(2,1)S(1)}, bf16[2,10,130,512]{3,2,1,0:T(8,128)(2,1)}, u32[]{:S(2)}) copy-start(bf16[2,10,130,512]{3,2,1,0:T(8,128)(2,1)} %gather_fusion) | copy-start | bytes 7987204
  201.1 4.9 %copy-start.17 = (bf16[2,8,128,512]{3,2,1,0:T(8,128)(2,1)S(1)}, bf16[2,8,128,512]{3,2,1,0:T(8,128)(2,1)}, u32[]{:S(2)}) copy-start(bf16[2,8,128,512]{3,2,1,0:T(8,128)(2,1)} %get-tuple-element.35) | copy-start | bytes 6291460
  201.1 4.9 %copy-start.18 = (bf16[2,8,128,512]{3,2,1,0:T(8,128)(2,1)S(1)}, bf16[2,8,128,512]{3,2,1,0:T(8,128)(2,1)}, u32[]{:S(2)}) copy-start(bf16[2,8,128,512]{3,2,1,0:T(8,128)(2,1)} %get-tuple-element.36) | copy-start | bytes 6291460
  201.1 4.9 %copy-start.19 = (bf16[2,8,128,512]{3,2,1,0:T(8,128)(2,1)S(1)}, bf16[2,8,128,512]{3,2,1,0:T(8,128)(2,1)}, u32[]{:S(2)}) copy-start(bf16[2,8,128,512]{3,2,1,0:T(8,128)(2,1)} %get-tuple-element.37) | copy-start | bytes 6291460
  210.5 4.9 %copy-start.2 = (bf16[2,8,128,512]{3,2,1,0:T(8,128)(2,1)S(1)}, bf16[2,8,128,512]{3,2,1,0:T(8,128)(2,1)}, u32[]{:S(2)}) copy-start(bf16[2,8,128,512]{3,2,1,0:T(8,128)(2,1)} %get-tuple-element.46) | copy-start | bytes 6291460
  221.7 4.9 %copy-start.14 = (bf16[2,8,128,512]{3,2,1,0:T(8,128)(2,1)S(1)}, bf16[2,8,128,512]{3,2,1,0:T(8,128)(2,1)}, u32[]{:S(2)}) copy-start(bf16[2,8,128,512]{3,2,1,0:T(8,128)(2,1)} %get-tuple-element.39) | copy-start | bytes 6291460
  221.7 4.9 %copy-start.15 = (bf16[2,8,128,512]{3,2,1,0:T(8,128)(2,1)S(1)}, bf16[2,8,128,512]{3,2,1,0:T(8,128)(2,1)}, u32[]{:S(2)}) copy-start(bf16[2,8,128,512]{3,2,1,0:T(8,128)(2,1)} %get-tuple-element.40) | copy-start | bytes 6291460
  221.7 4.9 %copy-start.16 = (bf16[2,8,128,512]{3,2,1,0:T(8,128)(2,1)S(1)}, bf16[2,8,128,512]{3,2,1,0:T(8,128)(2,1)}, u32[]{:S(2)}) copy-start(bf16[2,8,128,512]{3,2,1,0:T(8,128)(2,1)} %get-tuple-element.41) | copy-start | bytes 6291460
  230.9 4.9 %copy-start.11 = (bf16[2,8,128,512]{3,2,1,0:T(8,128)(2,1)S(1)}, bf16[2,8,128,512]{3,2,1,0:T(8,128)(2,1)}, u32[]{:S(2)}) copy-start(bf16[2,8,128,512]{3,2,1,0:T(8,128)(2,1)} %get-tuple-element.47) | copy-start | bytes 6291460
  230.9 4.9 %copy-start.12 = (bf16[2,8,128,512]{3,2,1,0:T(8,128)(2,1)S(1)}, bf16[2,8,128,512]{3,2,1,0:T(8,128)(2,1)}, u32[]{:S(2)}) copy-start(bf16[2,8,128,512]{3,2,1,0:T(8,128)(2,1)} %get-tuple-element.54) | copy-start | bytes 6291460
  230.9 4.9 %copy-start.13 = (bf16[2,8,128,512]{3,2,1,0:T(8,128)(2,1)S(1)}, bf16[2,8,128,512]{3,2,1,0:T(8,128)(2,1)}, u32[]{:S(2)}) copy-start(bf16[2,8,128,512]{3,2,1,0:T(8,128)(2,1)} %get-tuple-element.55) | copy-start | bytes 6291460
  240.1 5.0 %copy-start.8 = (bf16[2,8,128,512]{3,2,1,0:T(8,128)(2,1)S(1)}, bf16[2,8,128,512]{3,2,1,0:T(8,128)(2,1)}, u32[]{:S(2)}) copy-start(bf16[2,8,128,512]{3,2,1,0:T(8,128)(2,1)} %get-tuple-element.48) | copy-start | bytes 6291460
  240.1 5.0 %copy-start.9 = (bf16[2,8,128,512]{3,2,1,0:T(8,128)(2,1)S(1)}, bf16[2,8,128,512]{3,2,1,0:T(8,128)(2,1)}, u32[]{:S(2)}) copy-start(bf16[2,8,128,512]{3,2,1,0:T(8,128)(2,1)} %get-tuple-element.49) | copy-start | bytes 6291460
  240.1 5.0 %copy-start.10 = (bf16[2,8,128,512]{3,2,1,0:T(8,128)(2,1)S(1)}, bf16[2,8,128,512]{3,2,1,0:T(8,128)(2,1)}, u32[]{:S(2)}) copy-start(bf16[2,8,128,512]{3,2,1,0:T(8,128)(2,1)} %get-tuple-element.50) | copy-start | bytes 6291460
  249.3 5.0 %copy-start.6 = (bf16[2,8,128,512]{3,2,1,0:T(8,128)(2,1)S(1)}, bf16[2,8,128,512]{3,2,1,0:T(8,128)(2,1)}, u32[]{:S(2)}) copy-start(bf16[2,8,128,512]{3,2,1,0:T(8,128)(2,1)} %get-tuple-element.52) | copy-start | bytes 6291460
  249.3 4.9 %copy-start.7 = (bf16[2,8,128,512]{3,2,1,0:T(8,128)(2,1)S(1)}, bf16[2,8,128,512]{3,2,1,0:T(8,128)(2,1)}, u32[]{:S(2)}) copy-start(bf16[2,8,128,512]{3,2,1,0:T(8,128)(2,1)} %get-tuple-element.53) | copy-start | bytes 6291460
  258.8 5.0 %copy-start.3 = (bf16[2,8,128,512]{3,2,1,0:T(8,128)(2,1)S(1)}, bf16[2,8,128,512]{3,2,1,0:T(8,128)(2,1)}, u32[]{:S(2)}) copy-start(bf16[2,8,128,512]{3,2,1,0:T(8,128)(2,1)} %get-tuple-element.29) | copy-start | bytes 6291460
  258.8 5.0 %copy-start.4 = (bf16[2,8,128,512]{3,2,1,0:T(8,128)(2,1)S(1)}, bf16[2,8,128,512]{3,2,1,0:T(8,128)(2,1)}, u32[]{:S(2)}) copy-start(bf16[2,8,128,512]{3,2,1,0:T(8,128)(2,1)} %get-tuple-element.30) | copy-start | bytes 6291460
  258.8 5.0 %copy-start.5 = (bf16[2,8,128,512]{3,2,1,0:T(8,128)(2,1)S(1)}, bf16[2,8,128,512]{3,2,1,0:T(8,128)(2,1)}, u32[]{:S(2)}) copy-start(bf16[2,8,128,512]{3,2,1,0:T(8,128)(2,1)} %get-tuple-element.31) | copy-start | bytes 6291460
  268.0 14.8 %copy-start = (bf16[2,8,128,512]{3,2,1,0:T(8,128)(2,1)S(1)}, bf16[2,8,128,512]{3,2,1,0:T(8,128)(2,1)}, u32[]{:S(2)}) copy-start(bf16[2,8,128,512]{3,2,1,0:T(8,128)(2,1)} %param.8) | copy-start | bytes 6291460
  268.0 14.8 %copy-start.28 = (f32[512]{0:T(512)S(1)}, f32[512]{0:T(512)}, u32[]{:S(2)}) copy-start(f32[512]{0:T(512)} %param.13) | copy-start | bytes 6148
  (8 other events, 31.7 us)
where the time goes:
time: 288 us; the launch traced here: 287 us
  blocking collectives  65 us (23%)
  other arithmetic  56.8 us (20%)
  matrix products  54.9 us (19%)
  waiting for transfers between devices  54.7 us (19%)
  local copies, waits for them, and re-layouts  45.4 us (16%)
  starting transfers between devices  10 us (3%)
    psum x1, blocking collectives, finish_stats(): lax.psum((local_sums, local_squares), ('req', 'tile', 'span'))  65 us
    dot_general x9, matrix products, convolve(): jnp.dot(stacked.reshape(frame_count * row_count * col_count, 3 * channels...  54.1 us
    ppermute x1, waiting for transfers between devices, shifted(): return lax.ppermute(array, axis, pairs)  48.6 us
    concatenate x8, other arithmetic, convolve(): jnp.concatenate([chosen[:, row_tap:row_tap + row_count, col_tap:col_tap +...  30.7 us
    slice x3, local copies, waits for them, and re-layouts, convolve(): chosen[:, row_tap:row_tap + row_count, col_tap:col_tap + col_count]  21.8 us
    gather x3, local copies, waits for them, and re-layouts, convolve(): chosen = jnp.take(padded, tap_index[time_tap], axis=0)  13.1 us
    concatenate x1, other arithmetic, shards(): padded = jnp.pad(extended, ((0, 0), (0, 0), (1, 1), (0, 0)), mode='edge')  9.92 us
    slice x1, local copies, waits for them, and re-layouts, convolve(): kernel = conv_weight[time_tap, row_tap].reshape(3 * channels, channels)  9.58 us
  transfers between devices with their start and end apart: 3, of which 2 were waited for; matrix products, arithmetic and copies ran while one was open for 3% of the time, Pallas kernels for 0%

commit v1 on v0

--- a/solution.py
+++ b/solution.py
@@ -50,7 +50,9 @@
 
 
 def finish_stats(local_sums, local_squares, cell_count):
-    total_sums, total_squares = lax.psum((local_sums, local_squares), ("req", "tile", "span"))
+    total_sums, total_squares = lax.psum(
+        lax.psum((local_sums, local_squares), ("tile", "span")), "req"
+    )
     group_mean = total_sums / cell_count
     group_scale = lax.rsqrt(total_squares / cell_count - group_mean * group_mean + EPSILON)
     return (group_mean, group_scale)

time: 288 us -> 287 us (level); the launches traced: 287 us -> 283 us
  blocking collectives: 65 us -> 60.2 us
  starting transfers between devices: 10 us -> 13.8 us
  waiting for transfers between devices: 54.7 us -> 51.7 us
    psum x1 -> x2, blocking collectives: 65 us -> 60.2 us  [the longest x1 53.2 us: finish_stats(): lax.psum((local_sums, local_squares), ('tile', 'span'))]
    ppermute x1, starting transfers between devices: 4.42 us -> 8.15 us  [extended_2(): before = lax.ppermute(last, axis, up)]
    ppermute x1, waiting for transfers between devices: 48.6 us -> 45.6 us  [shifted(): return lax.ppermute(array, axis, pairs)]
where the time goes in v1:
time: 287 us; the launch traced here: 283 us
  blocking collectives  60.2 us (21%)
  other arithmetic  56.8 us (20%)
  matrix products  54.8 us (19%)
  waiting for transfers between devices  51.7 us (18%)
  local copies, waits for them, and re-layouts  45.4 us (16%)
  starting transfers between devices  13.8 us (5%)
    dot_general x9, matrix products, convolve(): jnp.dot(stacked.reshape(frame_count * row_count * col_count, 3 * channels...  54.1 us
    psum x1, blocking collectives, finish_stats(): lax.psum((local_sums, local_squares), ('tile', 'span'))  53.2 us
    ppermute x1, waiting for transfers between devices, shifted(): return lax.ppermute(array, axis, pairs)  45.6 us
    concatenate x8, other arithmetic, convolve(): jnp.concatenate([chosen[:, row_tap:row_tap + row_count, col_tap:col_tap +...  30.7 us
    slice x3, local copies, waits for them, and re-layouts, convolve(): chosen[:, row_tap:row_tap + row_count, col_tap:col_tap + col_count]  21.8 us
    gather x3, local copies, waits for them, and re-layouts, convolve(): chosen = jnp.take(padded, tap_index[time_tap], axis=0)  13.1 us
    concatenate x1, other arithmetic, shards(): padded = jnp.pad(extended, ((0, 0), (0, 0), (1, 1), (0, 0)), mode='edge')  9.91 us
    slice x1, local copies, waits for them, and re-layouts, convolve(): kernel = conv_weight[time_tap, row_tap].reshape(3 * channels, channels)  9.56 us
  transfers between devices with their start and end apart: 3, of which 2 were waited for; matrix products, arithmetic and copies ran while one was open for 3% of the time, Pallas kernels for 0%

profile of v1, /device:TPU:41, one launch (start us, length us, event | category | flops | bytes accessed | tf_op | source)
XLA Modules:
  0.0 283.1 jit_solution(17280928781474107687)
XLA Ops:
  4.6 53.2 %all-reduce = (f32[4,32]{1,0:T(4,128)S(1)}, f32[4,32]{1,0:T(4,128)S(1)}) all-reduce(f32[4,32]{1,0:T(4,128)S(1)} %fusion.40, f32[4,32]{1,0:T(4,128)S(1)} %fusion.39), channel_id=1, replica_groups=mesh['req'=4,'tile'=8,'span'=4] {'tile','span'}, use_global_device_ids=true, to_apply=%region_7.8 | all-reduce | flops 256 | bytes 2048 | tf_op jit(solution)/shard_map/psum | solution.py:54
  57.7 7.0 %all-reduce.1 = (f32[4,32]{1,0:T(4,128)S(1)}, f32[4,32]{1,0:T(4,128)S(1)}) all-reduce(f32[4,32]{1,0:T(4,128)S(1)} %get-tuple-element.8, f32[4,32]{1,0:T(4,128)S(1)} %get-tuple-element.9), channel_id=1, replica_groups=mesh['req'=4,'tile'=8,'span'=4] {'req'}, use_global_device_ids=true, to_apply=%region_8.9 | all-reduce | flops 256 | bytes 2048 | tf_op jit(solution)/shard_map/psum | solution.py:53
  70.5 45.6 %collective-permute-done = bf16[2,8,128,512]{3,2,1,0:T(8,128)(2,1)} collective-permute-done((bf16[2,8,128,512]{3,2,1,0:T(8,128)(2,1)S(1)}, bf16[2,8,128,512]{3,2,1,0:T(8,128)(2,1)}, u32[]{:S(2)}, u32[]{:S(2)}) %collective-permute-start) | collective-permute-done | bytes 2097184 | tf_op jit(solution)/shard_map/ppermute | solution.py:26
  117.1 8.1 %collective-permute-start.1 = (bf16[4,1,128,512]{3,2,1,0:T(8,128)(2,1)S(1)}, bf16[4,1,128,512]{3,2,1,0:T(8,128)(2,1)S(1)}, u32[]{:S(2)}, u32[]{:S(2)}) collective-permute-start(bf16[4,1,128,512]{3,2,1,0:T(8,128)(2,1)S(1)} %pad_maximum_fusion.9), channel_id=1, source_target_pairs={{0,4},{4,8},{8,12},{12,16},{16,20},{20,24},{24,28},{1,5},{5,9},{9,... | collective-permute-start | bytes 1572872 | tf_op jit(solution)/shard_map/ppermute | solution.py:17
  125.3 6.0 %collective-permute-done.1 = bf16[4,1,128,512]{3,2,1,0:T(8,128)(2,1)S(1)} collective-permute-done((bf16[4,1,128,512]{3,2,1,0:T(8,128)(2,1)S(1)}, bf16[4,1,128,512]{3,2,1,0:T(8,128)(2,1)S(1)}, u32[]{:S(2)}, u32[]{:S(2)}) %collective-permute-start.1) | collective-permute-done | bytes 524320 | tf_op jit(solution)/shard_map/ppermute | solution.py:17
  136.1 9.6 %fusion.35 = (bf16[1,1,3,512,512]{4,3,2,1,0:T(8,128)(2,1)}, bf16[1,1,3,512,512]{4,3,2,1,0:T(8,128)(2,1)}, bf16[1,1,3,512,512]{4,3,2,1,0:T(8,128)(2,1)}, bf16[1,1...) fusion(bf16[3,3,3,512,512]{4,3,2,1,0:T(8,128)(2,1)} %param.12), kind=kLoop, calls=%fused_computation.77 | loop fusion | bytes 28311552 | tf_op jit(solution)/shard_map/slice | solution.py:91
  145.7 9.9 %fusion.11 = bf16[4,10,130,512]{3,2,1,0:T(8,128)(2,1)} fusion(bf16[4,1,128,512]{3,2,1,0:T(8,128)(2,1)S(1)} %broadcast_select_fusion.3, bf16[4,1,128,512]{3,2,1,0:T(8,128)(2,1)S(1)} %get-tuple-element.20, bf16[2,8,128,512]{3,2,1,0:T(8,128)(2,1)S(1)} %fusion.24, bf16[2,8,128,512]{3,2,1,0:T(8,128)(2,1)} %collective-permute-done), kind=kLoop, calls=%fused_computation.29 | loop fusion | flops 90521600 | bytes 10567680 | tf_op jit(solution)/shard_map/jit(_pad)/concatenate | solution.py:131
  159.0 4.9 %gather_fusion.1 = bf16[2,10,130,512]{3,2,1,0:T(8,128)(2,1)} fusion(bf16[4,10,130,512]{3,2,1,0:T(8,128)(2,1)} %fusion.11, s32[1024]{0:T(1024)S(1)} %pad_clamp_fusion.1), kind=kCustom, calls=%fused_computation.1.clone | custom fusion | bytes 5324808 | tf_op jit(solution)/shard_map/jit(_take)/gather | solution.py:82
  163.9 4.9 %gather_fusion = bf16[2,10,130,512]{3,2,1,0:T(8,128)(2,1)} fusion(bf16[4,10,130,512]{3,2,1,0:T(8,128)(2,1)} %fusion.11, s32[1024]{0:T(1024)S(1)} %pad_clamp_fusion.2), kind=kCustom, calls=%fused_computation.clone | custom fusion | bytes 5324808 | tf_op jit(solution)/shard_map/jit(_take)/gather | solution.py:82
  171.1 8.0 %fusion.36 = (bf16[2,8,128,512]{3,2,1,0:T(8,128)(2,1)}, bf16[2,8,128,512]{3,2,1,0:T(8,128)(2,1)}, bf16[2,8,128,512]{3,2,1,0:T(8,128)(2,1)}, bf16[2,8,128,512]{3,...) fusion(bf16[2,10,130,512]{3,2,1,0:T(8,128)(2,1)S(1)} %get-tuple, ...), kind=kLoop, calls=%fused_computation.78 | loop fusion | bytes 37748736 | tf_op jit(solution)/shard_map/slice | solution.py:86
  179.4 6.8 %fusion.37 = (bf16[2,8,128,512]{3,2,1,0:T(8,128)(2,1)S(1)}, bf16[2,8,128,512]{3,2,1,0:T(8,128)(2,1)}, bf16[2,8,128,512]{3,2,1,0:T(8,128)(2,1)}, bf16[2,8,128,512...) fusion(bf16[2,10,130,512]{3,2,1,0:T(8,128)(2,1)S(1)} %broadcast, ...), kind=kLoop, calls=%fused_computation.79 | loop fusion | bytes 37748736 | tf_op jit(solution)/shard_map/slice | solution.py:86
  186.2 7.1 %fusion.38 = (bf16[2,8,128,512]{3,2,1,0:T(8,128)(2,1)}, bf16[2,8,128,512]{3,2,1,0:T(8,128)(2,1)}, bf16[2,8,128,512]{3,2,1,0:T(8,128)(2,1)}, bf16[2,8,128,512]{3,...) fusion(bf16[2,10,130,512]{3,2,1,0:T(8,128)(2,1)S(1)} %get-tuple, ...), kind=kLoop, calls=%fused_computation.80 | loop fusion | bytes 37748736 | tf_op jit(solution)/shard_map/slice | solution.py:86
  197.0 4.9 %fusion.48 = f32[2048,512]{1,0:T(8,128)} fusion(bf16[2048,1536]{1,0:T(8,128)(2,1)S(1)} %bitcast.49, bf16[1536,512]{1,0:T(8,128)(2,1)S(1)} %bitcast.64), kind=kOutput, calls=%fused_computation.90 | convolution fusion | flops 3221225472 | bytes 12058624 | tf_op jit(solution)/shard_map/dot_general | solution.py:92
  201.9 4.4 %pad_maximum_fusion.6 = bf16[2,8,128,1536]{3,2,1,0:T(8,128)(2,1)S(1)} fusion(bf16[2,8,128,512]{3,2,1,0:T(8,128)(2,1)S(1)} %copy-done.17, bf16[2,8,128,512]{3,2,1,0:T(8,128)(2,1)S(1)} %copy-done.18, bf16[2,8,128,512]{3,2,1,0:T(8,128)(2,1)S(1)} %copy-done.19), kind=kLoop, calls=%fused_computation.23 | loop fusion | flops 18874368 | bytes 12582912 | tf_op jit(solution)/shard_map/concatenate | solution.py:84
  206.4 4.9 %fusion.47 = f32[2048,512]{1,0:T(8,128)} fusion(bf16[2048,1536]{1,0:T(8,128)(2,1)S(1)} %bitcast.50, bf16[1536,512]{1,0:T(8,128)(2,1)S(1)} %bitcast.63), kind=kOutput, calls=%fused_computation.89 | convolution fusion | flops 3221225472 | bytes 12058624 | tf_op jit(solution)/shard_map/dot_general | solution.py:92
  212.7 4.9 %fusion.41 = f32[2048,512]{1,0:T(8,128)} fusion(bf16[2048,1536]{1,0:T(8,128)(2,1)S(1)} %bitcast.56, bf16[1536,512]{1,0:T(8,128)(2,1)S(1)} %bitcast.62), kind=kOutput, calls=%fused_computation.83 | convolution fusion | flops 3221225472 | bytes 12058624 | tf_op jit(solution)/shard_map/dot_general | solution.py:92
  217.6 4.9 %fusion.42 = f32[2048,512]{1,0:T(8,128)} fusion(bf16[2048,1536]{1,0:T(8,128)(2,1)S(1)} %bitcast.55, bf16[1536,512]{1,0:T(8,128)(2,1)S(1)} %bitcast.61), kind=kOutput, calls=%fused_computation.84 | convolution fusion | flops 3221225472 | bytes 12058624 | tf_op jit(solution)/shard_map/dot_general | solution.py:92
  226.8 4.9 %fusion.43 = f32[2048,512]{1,0:T(8,128)} fusion(bf16[2048,1536]{1,0:T(8,128)(2,1)S(1)} %bitcast.51, bf16[1536,512]{1,0:T(8,128)(2,1)S(1)} %bitcast.60), kind=kOutput, calls=%fused_computation.85 | convolution fusion | flops 3221225472 | bytes 12058624 | tf_op jit(solution)/shard_map/dot_general | solution.py:92
  236.0 5.0 %fusion.44 = f32[2048,512]{1,0:T(8,128)} fusion(bf16[2048,1536]{1,0:T(8,128)(2,1)S(1)} %bitcast.52, bf16[1536,512]{1,0:T(8,128)(2,1)S(1)} %bitcast.59), kind=kOutput, calls=%fused_computation.86 | convolution fusion | flops 3221225472 | bytes 12058624 | tf_op jit(solution)/shard_map/dot_general | solution.py:92
  245.2 4.9 %fusion.46 = f32[2048,512]{1,0:T(8,128)} fusion(bf16[2048,1536]{1,0:T(8,128)(2,1)S(1)} %bitcast.53, bf16[1536,512]{1,0:T(8,128)(2,1)S(1)} %bitcast.58), kind=kOutput, calls=%fused_computation.88 | convolution fusion | flops 3221225472 | bytes 12058624 | tf_op jit(solution)/shard_map/dot_general | solution.py:92
  250.2 4.5 %pad_maximum_fusion.4 = bf16[2,8,128,1536]{3,2,1,0:T(8,128)(2,1)S(1)} fusion(bf16[2,8,128,512]{3,2,1,0:T(8,128)(2,1)S(1)} %get-tuple-element.53, bf16[2,8,128,512]{3,2,1,0:T(8,128)(2,1)S(1)} %copy-done.6, bf16[2,8,128,512]{3,2,1,0:T(8,128)(2,1)S(1)} %copy-done.7), kind=kLoop, calls=%fused_computation.21 | loop fusion | flops 18874368 | bytes 12582912 | tf_op jit(solution)/shard_map/concatenate | solution.py:84
  254.7 5.0 %fusion.45 = f32[2048,512]{1,0:T(8,128)} fusion(bf16[2048,1536]{1,0:T(8,128)(2,1)S(1)} %bitcast.54, bf16[1536,512]{1,0:T(8,128)(2,1)S(1)} %bitcast.57), kind=kOutput, calls=%fused_computation.87 | convolution fusion | flops 3221225472 | bytes 12058624 | tf_op jit(solution)/shard_map/dot_general | solution.py:92
  263.9 14.8 %add_add_fusion = f32[2048,512]{1,0:T(8,128)} fusion(f32[2048,512]{1,0:T(8,128)} %fusion.48, f32[2048,512]{1,0:T(8,128)} %fusion.47, f32[2048,512]{1,0:T(8,128)} %fusion.46, f32[2048,512]{1,0:T(8,128)} %fusion.45, f32[2048,512]{1,0:T(8,128)} %fusion.44, f32[2048,512]{1,0:T(8,128)} %fusion.43, f32[2048,512]{1,0:T(8,128)} %fusion.41, ...), kind=kOutput, calls=%fused_computation.46 | convolution fusion | flops 3229614080 | bytes 45613056 | tf_op jit(solution)/shard_map/dot_general | solution.py:92
  278.7 4.4 %fusion.27 = bf16[2,8,128,512]{3,2,1,0:T(8,128)(2,1)} fusion(f32[2,8,128,512]{3,2,1,0:T(8,128)} %bitcast.47, bf16[2,8,128,512]{3,2,1,0:T(8,128)(2,1)S(1)} %copy-done, f32[512]{0:T(512)S(1)} %copy-done.28), kind=kLoop, calls=%fused_computation.45 | loop fusion | flops 4194304 | bytes 8390656 | tf_op jit(solution)/shard_map/convert_element_type | solution.py:141
  (95 shorter events, 44.1 us)
Async XLA Ops:
  68.5 47.6 %collective-permute-start = (bf16[2,8,128,512]{3,2,1,0:T(8,128)(2,1)S(1)}, bf16[2,8,128,512]{3,2,1,0:T(8,128)(2,1)}, u32[]{:S(2)}, u32[]{:S(2)}) collective-permute-start(bf16[2,8,128,512]{3,2,1,0:T(8,128)(2,1)S(1)} %fusion.24), channel_id=1, source_target_pairs={{0,1},{1,2},{2,3},{3,32},{32,33},{33,34},{34,35},{35,64},{64,65},{... | collective-permute-start | bytes 6291464 | tf_op jit(solution)/shard_map/ppermute | solution.py:26
  117.1 14.3 %collective-permute-start.1 = (bf16[4,1,128,512]{3,2,1,0:T(8,128)(2,1)S(1)}, bf16[4,1,128,512]{3,2,1,0:T(8,128)(2,1)S(1)}, u32[]{:S(2)}, u32[]{:S(2)}) collective-permute-start(bf16[4,1,128,512]{3,2,1,0:T(8,128)(2,1)S(1)} %pad_maximum_fusion.9), channel_id=1, source_target_pairs={{0,4},{4,8},{8,12},{12,16},{16,20},{20,24},{24,28},{1,5},{5,9},{9,... | collective-permute-start | bytes 1572872 | tf_op jit(solution)/shard_map/ppermute | solution.py:17
  132.4 13.3 %collective-permute-start.2 = (bf16[4,1,128,512]{3,2,1,0:T(8,128)(2,1)S(1)}, bf16[4,1,128,512]{3,2,1,0:T(8,128)(2,1)S(1)}, u32[]{:S(2)}, u32[]{:S(2)}) collective-permute-start(bf16[4,1,128,512]{3,2,1,0:T(8,128)(2,1)S(1)} %get-tuple-element.21), channel_id=1, source_target_pairs={{4,0},{8,4},{12,8},{16,12},{20,16},{24,20},{28,24},{5,1},{9,5},{13... | collective-permute-start | bytes 1572872 | tf_op jit(solution)/shard_map/ppermute | solution.py:18
  171.1 8.0 %copy-start.1 = (bf16[2,10,130,512]{3,2,1,0:T(8,128)(2,1)S(1)}, bf16[2,10,130,512]{3,2,1,0:T(8,128)(2,1)}, u32[]{:S(2)}) copy-start(bf16[2,10,130,512]{3,2,1,0:T(8,128)(2,1)} %gather_fusion) | copy-start | bytes 7987204
  197.0 4.9 %copy-start.17 = (bf16[2,8,128,512]{3,2,1,0:T(8,128)(2,1)S(1)}, bf16[2,8,128,512]{3,2,1,0:T(8,128)(2,1)}, u32[]{:S(2)}) copy-start(bf16[2,8,128,512]{3,2,1,0:T(8,128)(2,1)} %get-tuple-element.37) | copy-start | bytes 6291460
  197.0 4.9 %copy-start.18 = (bf16[2,8,128,512]{3,2,1,0:T(8,128)(2,1)S(1)}, bf16[2,8,128,512]{3,2,1,0:T(8,128)(2,1)}, u32[]{:S(2)}) copy-start(bf16[2,8,128,512]{3,2,1,0:T(8,128)(2,1)} %get-tuple-element.38) | copy-start | bytes 6291460
  197.0 4.9 %copy-start.19 = (bf16[2,8,128,512]{3,2,1,0:T(8,128)(2,1)S(1)}, bf16[2,8,128,512]{3,2,1,0:T(8,128)(2,1)}, u32[]{:S(2)}) copy-start(bf16[2,8,128,512]{3,2,1,0:T(8,128)(2,1)} %get-tuple-element.39) | copy-start | bytes 6291460
  206.4 4.9 %copy-start.2 = (bf16[2,8,128,512]{3,2,1,0:T(8,128)(2,1)S(1)}, bf16[2,8,128,512]{3,2,1,0:T(8,128)(2,1)}, u32[]{:S(2)}) copy-start(bf16[2,8,128,512]{3,2,1,0:T(8,128)(2,1)} %get-tuple-element.48) | copy-start | bytes 6291460
  217.6 4.9 %copy-start.14 = (bf16[2,8,128,512]{3,2,1,0:T(8,128)(2,1)S(1)}, bf16[2,8,128,512]{3,2,1,0:T(8,128)(2,1)}, u32[]{:S(2)}) copy-start(bf16[2,8,128,512]{3,2,1,0:T(8,128)(2,1)} %get-tuple-element.41) | copy-start | bytes 6291460
  217.6 4.9 %copy-start.15 = (bf16[2,8,128,512]{3,2,1,0:T(8,128)(2,1)S(1)}, bf16[2,8,128,512]{3,2,1,0:T(8,128)(2,1)}, u32[]{:S(2)}) copy-start(bf16[2,8,128,512]{3,2,1,0:T(8,128)(2,1)} %get-tuple-element.42) | copy-start | bytes 6291460
  217.6 4.9 %copy-start.16 = (bf16[2,8,128,512]{3,2,1,0:T(8,128)(2,1)S(1)}, bf16[2,8,128,512]{3,2,1,0:T(8,128)(2,1)}, u32[]{:S(2)}) copy-start(bf16[2,8,128,512]{3,2,1,0:T(8,128)(2,1)} %get-tuple-element.43) | copy-start | bytes 6291460
  226.8 4.9 %copy-start.11 = (bf16[2,8,128,512]{3,2,1,0:T(8,128)(2,1)S(1)}, bf16[2,8,128,512]{3,2,1,0:T(8,128)(2,1)}, u32[]{:S(2)}) copy-start(bf16[2,8,128,512]{3,2,1,0:T(8,128)(2,1)} %get-tuple-element.49) | copy-start | bytes 6291460
  226.8 4.9 %copy-start.12 = (bf16[2,8,128,512]{3,2,1,0:T(8,128)(2,1)S(1)}, bf16[2,8,128,512]{3,2,1,0:T(8,128)(2,1)}, u32[]{:S(2)}) copy-start(bf16[2,8,128,512]{3,2,1,0:T(8,128)(2,1)} %get-tuple-element.56) | copy-start | bytes 6291460
  226.8 4.9 %copy-start.13 = (bf16[2,8,128,512]{3,2,1,0:T(8,128)(2,1)S(1)}, bf16[2,8,128,512]{3,2,1,0:T(8,128)(2,1)}, u32[]{:S(2)}) copy-start(bf16[2,8,128,512]{3,2,1,0:T(8,128)(2,1)} %get-tuple-element.57) | copy-start | bytes 6291460
  236.0 5.0 %copy-start.8 = (bf16[2,8,128,512]{3,2,1,0:T(8,128)(2,1)S(1)}, bf16[2,8,128,512]{3,2,1,0:T(8,128)(2,1)}, u32[]{:S(2)}) copy-start(bf16[2,8,128,512]{3,2,1,0:T(8,128)(2,1)} %get-tuple-element.50) | copy-start | bytes 6291460
  236.0 5.0 %copy-start.9 = (bf16[2,8,128,512]{3,2,1,0:T(8,128)(2,1)S(1)}, bf16[2,8,128,512]{3,2,1,0:T(8,128)(2,1)}, u32[]{:S(2)}) copy-start(bf16[2,8,128,512]{3,2,1,0:T(8,128)(2,1)} %get-tuple-element.51) | copy-start | bytes 6291460
  236.0 5.0 %copy-start.10 = (bf16[2,8,128,512]{3,2,1,0:T(8,128)(2,1)S(1)}, bf16[2,8,128,512]{3,2,1,0:T(8,128)(2,1)}, u32[]{:S(2)}) copy-start(bf16[2,8,128,512]{3,2,1,0:T(8,128)(2,1)} %get-tuple-element.52) | copy-start | bytes 6291460
  245.2 5.0 %copy-start.6 = (bf16[2,8,128,512]{3,2,1,0:T(8,128)(2,1)S(1)}, bf16[2,8,128,512]{3,2,1,0:T(8,128)(2,1)}, u32[]{:S(2)}) copy-start(bf16[2,8,128,512]{3,2,1,0:T(8,128)(2,1)} %get-tuple-element.54) | copy-start | bytes 6291460
  245.2 4.9 %copy-start.7 = (bf16[2,8,128,512]{3,2,1,0:T(8,128)(2,1)S(1)}, bf16[2,8,128,512]{3,2,1,0:T(8,128)(2,1)}, u32[]{:S(2)}) copy-start(bf16[2,8,128,512]{3,2,1,0:T(8,128)(2,1)} %get-tuple-element.55) | copy-start | bytes 6291460
  254.7 5.0 %copy-start.3 = (bf16[2,8,128,512]{3,2,1,0:T(8,128)(2,1)S(1)}, bf16[2,8,128,512]{3,2,1,0:T(8,128)(2,1)}, u32[]{:S(2)}) copy-start(bf16[2,8,128,512]{3,2,1,0:T(8,128)(2,1)} %get-tuple-element.31) | copy-start | bytes 6291460
  254.7 5.0 %copy-start.4 = (bf16[2,8,128,512]{3,2,1,0:T(8,128)(2,1)S(1)}, bf16[2,8,128,512]{3,2,1,0:T(8,128)(2,1)}, u32[]{:S(2)}) copy-start(bf16[2,8,128,512]{3,2,1,0:T(8,128)(2,1)} %get-tuple-element.32) | copy-start | bytes 6291460
  254.7 5.0 %copy-start.5 = (bf16[2,8,128,512]{3,2,1,0:T(8,128)(2,1)S(1)}, bf16[2,8,128,512]{3,2,1,0:T(8,128)(2,1)}, u32[]{:S(2)}) copy-start(bf16[2,8,128,512]{3,2,1,0:T(8,128)(2,1)} %get-tuple-element.33) | copy-start | bytes 6291460
  263.9 14.8 %copy-start = (bf16[2,8,128,512]{3,2,1,0:T(8,128)(2,1)S(1)}, bf16[2,8,128,512]{3,2,1,0:T(8,128)(2,1)}, u32[]{:S(2)}) copy-start(bf16[2,8,128,512]{3,2,1,0:T(8,128)(2,1)} %param.8) | copy-start | bytes 6291460
  263.9 14.8 %copy-start.28 = (f32[512]{0:T(512)S(1)}, f32[512]{0:T(512)}, u32[]{:S(2)}) copy-start(f32[512]{0:T(512)} %param.13) | copy-start | bytes 6148
  (8 other events, 31.7 us)
